TPU v7x, 32 devices: a whole 2x2x4 slice. The times are simulated.
32 devices in a mesh: tile: 16 (over z, x, core), group: 2 (over y).
Axes of the slice: x: 2, y: 2, z: 4, core: 2. Of those that a mesh axis runs over, the one named last changes fastest.
Arguments:
- object_field: float32 [2, 320, 2048], P(None, 'group', 'tile'), may hold values from -6 to 6
- probe_field: float32 [2, 256, 256], replicated, may hold values from -6 to 6
- amplitudes: float32 [32, 256, 256], P(('tile', 'group')), may hold values from 0 to 4
- row_start: int32 [32], P(('tile', 'group')), may hold values from 0 to 64
- column_start: int32 [32], P(('tile', 'group')), may hold values from 0 to 128
- live_slots: int32 [32], P(('tile', 'group')), may hold values 0 or 1
Outputs:
- new_object: float32 [2, 320, 2048], P(None, 'group', 'tile')
- new_probe: float32 [2, 256, 256], replicated
All inputs are finite; a program needn't handle non-finite values. No bound on the sum of `live_slots` on one device may be relied on, other than what follows from the above.
Results may differ from a plain program's by a relative error of at most 0.0001.
Values sent between devices are 32-bit elements; how exact they have to be, the bound alone decides.
A program may use at most 64 MiB of HBM per device.

v0:
```python
import math

import jax
import jax.numpy as jnp
from jax import lax
from jax.sharding import PartitionSpec as P

WIN = 256
HALO = 128


def padded_2(value, sides, width):
    for axis, dim in sides:
        count, length = (lax.axis_size(axis), value.shape[dim])
        up = [(i, (i + 1) % count) for i in range(count - 1)]
        down = [(j, i) for i, j in up]
        last = lax.slice_in_dim(value, length - width, length, axis=dim)
        initial = lax.slice_in_dim(value, 0, width, axis=dim)
        before = lax.ppermute(last, axis, up)
        after = lax.ppermute(initial, axis, down)
        value = jnp.concatenate([before, value, after], axis=dim)
    return value


def dft_tables(length):
    counter = jnp.arange(length, dtype=jnp.int32)
    product = counter[:, None] * counter[None, :] % length
    angles = 2.0 * math.pi / length * product.astype(jnp.float32)
    factor = 1.0 / math.sqrt(length)
    return (jnp.cos(angles) * factor, jnp.sin(angles) * factor)


def apply_left(matrix, values):
    return jnp.einsum("jk,pkl->pjl", matrix, values, precision=lax.Precision.HIGHEST)


def apply_right(values, matrix):
    return jnp.einsum("pjk,kl->pjl", values, matrix, precision=lax.Precision.HIGHEST)


def transform(real_part, imag_part, cos_table, sin_table, sign):
    left_real = apply_left(cos_table, real_part) - sign * apply_left(sin_table, imag_part)
    left_imag = apply_left(cos_table, imag_part) + sign * apply_left(sin_table, real_part)
    right_real = apply_right(left_real, cos_table) - sign * apply_right(left_imag, sin_table)
    right_imag = apply_right(left_imag, cos_table) + sign * apply_right(left_real, sin_table)
    return (right_real, right_imag)


def window_terms(windows, probe_field, amplitudes, live_slots, cos_table, sin_table):
    sample_real = windows[:, 0]
    sample_imag = windows[:, 1]
    probe_real = probe_field[0]
    probe_imag = probe_field[1]
    exit_real = probe_real * sample_real - probe_imag * sample_imag
    exit_imag = probe_real * sample_imag + probe_imag * sample_real
    far_real, far_imag = transform(exit_real, exit_imag, cos_table, sin_table, -1.0)
    modulus = jnp.maximum(jnp.sqrt(far_real * far_real + far_imag * far_imag), 0.25)
    factor = 1.0 - amplitudes / modulus
    miss_real, miss_imag = transform(
        far_real * factor, far_imag * factor, cos_table, sin_table, 1.0
    )
    weight = live_slots.astype(jnp.float32)[:, None, None]
    miss_real = miss_real * weight
    miss_imag = miss_imag * weight
    grad_real = probe_real * miss_real + probe_imag * miss_imag
    grad_imag = probe_real * miss_imag - probe_imag * miss_real
    probe_light = weight * (probe_real * probe_real + probe_imag * probe_imag)
    terms = jnp.stack([grad_real, grad_imag, probe_light], axis=1)
    probe_grad = jnp.stack(
        [
            jnp.sum(sample_real * miss_real + sample_imag * miss_imag, axis=0),
            jnp.sum(sample_real * miss_imag - sample_imag * miss_real, axis=0),
        ],
        axis=0,
    )
    window_light = jnp.sum(weight * (sample_real * sample_real + sample_imag * sample_imag), axis=0)
    return (terms, probe_grad, window_light)


def add_windows(accum, terms, top_rows, left_edges):
    zero_index = jnp.zeros((), jnp.int32)
    channels = terms.shape[1]

    def place(slot, current):
        corner = (zero_index, top_rows[slot], left_edges[slot])
        piece = lax.dynamic_slice(current, corner, (channels, WIN, WIN))
        return lax.dynamic_update_slice(current, piece + terms[slot], corner)

    return lax.fori_loop(0, terms.shape[0], place, accum)


def cut_windows(padded, top_rows, left_edges):
    zero_index = jnp.zeros((), jnp.int32)

    def single(top_row, left_edge):
        return lax.dynamic_slice(padded, (zero_index, top_row, left_edge), (2, WIN, WIN))

    return jax.vmap(single)(top_rows, left_edges)


def edge_strips(accum):
    return jnp.concatenate([accum[:, :, :HALO], accum[:, :, accum.shape[2] - HALO :]], axis=2)


def add_edges(inner, arrived):
    width = inner.shape[2]
    inner = inner.at[:, :, :HALO].add(arrived[:, :, :HALO])
    return inner.at[:, :, width - HALO :].add(arrived[:, :, arrived.shape[2] - HALO :])


def apply_updates(object_field, probe_field, share, probe_grad, window_light):
    light_max = jnp.max(probe_field[0] * probe_field[0] + probe_field[1] * probe_field[1]) + 1e-06
    new_object = object_field - share[0:2] / (share[2:3] + 0.25 * light_max)
    new_probe = (
        probe_field - probe_grad / (window_light + 0.25 * jnp.mean(window_light) + 1e-05)[None]
    )
    return (new_object, new_probe)


def local(object_field, probe_field, amplitudes, row_start, column_start, live_slots):
    cos_table, sin_table = dft_tables(WIN)
    full_rows = lax.all_gather(object_field, "group", axis=1, tiled=True)
    padded = padded_2(full_rows, (("tile", 2),), HALO)
    windows = cut_windows(padded, row_start, column_start)
    terms, probe_grad, window_light = window_terms(
        windows, probe_field, amplitudes, live_slots, cos_table, sin_table
    )
    accum = jnp.zeros((terms.shape[1], padded.shape[1], padded.shape[2]), jnp.float32)
    accum = add_windows(accum, terms, row_start, column_start)
    reduced = lax.psum_scatter(accum, "group", scatter_dimension=1, tiled=True)
    arrived = padded_2(edge_strips(reduced), (("tile", 2),), HALO)
    share = add_edges(reduced[:, :, HALO : reduced.shape[2] - HALO], arrived)
    probe_grad, window_light = lax.psum((probe_grad, window_light), ("tile", "group"))
    object_field, probe_field = apply_updates(
        object_field, probe_field, share, probe_grad, window_light
    )
    return (object_field, probe_field)


def solution(mesh):
    return jax.shard_map(
        local,
        mesh=mesh,
        in_specs=(
            P(None, "group", "tile"),
            P(),
            P(("tile", "group"), None, None),
            P(("tile", "group")),
            P(("tile", "group")),
            P(("tile", "group")),
        ),
        out_specs=(P(None, "group", "tile"), P()),
        check_vma=False,
    )
```

profile of v0, /device:TPU:3, one launch (start us, length us, event | category | flops | bytes accessed | tf_op | source)
XLA Modules:
  0.0 210.1 jit_solution(13786938275999001730)
XLA Ops:
  8.0 0.0 all-reduce.3.cloned.1.call-start
  8.1 6.1 %all_gather.3 = f32[2,320,128]{2,1,0:T(8,128)S(1)} all-gather(f32[2,160,128]{2,1,0:T(8,128)} %param.14), channel_id=1, replica_groups=mesh['tile'=16,'group'=2] {'group'}, dimensions={1}, use_global_device_ids=true | all-gather | bytes 491520 | tf_op jit(solution)/shard_map/all_gather | solution.py:122
  14.1 3.4 %collective-permute-start.1 = (f32[2,320,128]{2,1,0:T(8,128)S(1)}, f32[2,320,128]{2,1,0:T(8,128)S(1)}, u32[]{:S(2)}, u32[]{:S(2)}) collective-permute-start(f32[2,320,128]{2,1,0:T(8,128)S(1)} %all_gather.3), channel_id=1, source_target_pairs={{2,0},{4,2},{6,4},{8,6},{10,8},{12,10},{14,12},{16,14},{18,16},{20... | collective-permute-start | bytes 983048 | tf_op jit(solution)/shard_map/ppermute | solution.py:20
  17.6 3.1 %collective-permute-start = (f32[2,320,128]{2,1,0:T(8,128)S(1)}, f32[2,320,128]{2,1,0:T(8,128)S(1)}, u32[]{:S(2)}, u32[]{:S(2)}) collective-permute-start(f32[2,320,128]{2,1,0:T(8,128)S(1)} %all_gather.3), channel_id=1, source_target_pairs={{0,2},{2,4},{4,6},{6,8},{8,10},{10,12},{12,14},{14,16},{16,18},{18... | collective-permute-start | bytes 983048 | tf_op jit(solution)/shard_map/ppermute | solution.py:19
  22.6 1.0 collective-permute-done.1
  23.6 1.1 collective-permute-done
  24.7 0.4 fusion.12
  25.1 0.1 fusion.39
  25.2 1.5 fusion.37
  26.7 1.5 fusion.33
  28.2 1.5 fusion.9
  29.6 1.5 fusion.7
  31.1 1.5 fusion.48
  32.6 0.0 copy-start.4
  32.6 1.5 fusion.49
  34.1 1.5 fusion.4
  35.6 1.7 bitcast_multiply_fusion.11
  37.4 1.5 fusion.30
  38.8 1.5 fusion.26
  40.3 1.5 fusion.3
  41.8 1.5 fusion.2
  43.3 1.5 fusion.46
  44.8 1.5 fusion.47
  46.3 1.5 fusion
  47.8 1.7 fusion.1
  49.5 0.8 fusion.17
  50.3 0.8 pad_maximum_fusion
  51.1 0.0 all-reduce.3.cloned.1.call-update
  51.1 0.0 reduce-scatter.2.cloned.1.call-start
  51.2 0.7 fusion.23
  51.9 0.1 maximum_bitcast_fusion
  51.9 0.1 broadcast_in_dim.6
  52.0 10.7 %dynamic_update_slice.4 = f32[3,320,384]{2,1,0:T(8,128)S(1)} dynamic-update-slice(f32[3,320,384]{2,1,0:T(8,128)S(1)} %broadcast_in_dim.6, f32[3,256,256]{2,1,0:T(8,128)S(1)} %maximum_bitcast_fusion, s32[]{:T(128)} %constant.112.clone.1, s32[]{:T(128)S(6)} %select_n.60, s32[]{:T(128)S(6)} %select_n.61) | dynamic-update-slice | bytes 1572868 | tf_op jit(solution)/shard_map/while/body/eval_jaxpr/dynamic_update_slice | solution.py:87
  62.8 1.1 copy-done
  63.9 0.0 reduce-scatter.2.cloned.1.call-update
  64.6 119.0 %all-reduce.3.cloned.1.call-done = (f32[2,256,256]{2,1,0:T(8,128)}, f32[256,256]{1,0:T(8,128)}) async-done(((f32[2,256,256]{2,1,0:T(8,128)}, f32[256,256]{1,0:T(8,128)}), (f32[2,256,256]{2,1,0:T(8,128)}, f32[256,256]{1,0:T(8,128)})) %all-reduce.3.cloned.1.call-update) | async-done | bytes 786448 | tf_op jit(solution)/shard_map/psum | solution.py:133
  183.6 1.7 reduce_sum.8
  186.0 1.0 add_add_fusion
  187.0 0.0 reduce-scatter.2.cloned.1.call-done
  187.0 1.1 fusion.132
  188.1 4.5 %collective-permute-start.2 = (f32[3,160,128]{2,1,0:T(8,128)S(1)}, f32[3,160,128]{2,1,0:T(8,128)S(1)}, u32[]{:S(2)}, u32[]{:S(2)}) collective-permute-start(f32[3,160,128]{2,1,0:T(8,128)S(1)} %get-tuple-element.81), channel_id=1, source_target_pairs={{0,2},{2,4},{4,6},{6,8},{8,10},{10,12},{12,14},{14,16},{16,18},{18... | collective-permute-start | bytes 737288 | tf_op jit(solution)/shard_map/ppermute | solution.py:19
  192.6 1.9 collective-permute-start.3
  194.5 0.0 copy-start.2
  194.5 0.9 divide_subtract_fusion
  195.4 0.3 collective-permute-done.2
  195.7 5.3 %collective-permute-done.3 = f32[3,160,128]{2,1,0:T(8,128)S(1)} collective-permute-done((f32[3,160,128]{2,1,0:T(8,128)S(1)}, f32[3,160,128]{2,1,0:T(8,128)S(1)}, u32[]{:S(2)}, u32[]{:S(2)}) %collective-permute-start.3) | collective-permute-done | bytes 245792 | tf_op jit(solution)/shard_map/ppermute | solution.py:20
  201.0 1.0 fusion.44
  202.0 0.7 fusion.45
  (8 shorter events, 0.0 us)
Async XLA Ops:
  8.0 17.1 %copy-start.1 = (f32[2,256,256]{2,1,0:T(8,128)S(1)}, f32[2,256,256]{2,1,0:T(8,128)}, u32[]{:S(2)}) copy-start(f32[2,256,256]{2,1,0:T(8,128)} %param.15) | copy-start | bytes 1572868
  8.0 175.6 %all-reduce.3.cloned.1.call-start = ((), (), s32[]{:S(2)}) async-start(), calls=%async_computation.2 | async-start | bytes 1572864 | tf_op jit(solution)/shard_map/psum | solution.py:133
  14.1 9.4 %collective-permute-start.1 = (f32[2,320,128]{2,1,0:T(8,128)S(1)}, f32[2,320,128]{2,1,0:T(8,128)S(1)}, u32[]{:S(2)}, u32[]{:S(2)}) collective-permute-start(f32[2,320,128]{2,1,0:T(8,128)S(1)} %all_gather.3), channel_id=1, source_target_pairs={{2,0},{4,2},{6,4},{8,6},{10,8},{12,10},{14,12},{16,14},{18,16},{20... | collective-permute-start | bytes 983048 | tf_op jit(solution)/shard_map/ppermute | solution.py:20
  17.6 7.1 %collective-permute-start = (f32[2,320,128]{2,1,0:T(8,128)S(1)}, f32[2,320,128]{2,1,0:T(8,128)S(1)}, u32[]{:S(2)}, u32[]{:S(2)}) collective-permute-start(f32[2,320,128]{2,1,0:T(8,128)S(1)} %all_gather.3), channel_id=1, source_target_pairs={{0,2},{2,4},{4,6},{6,8},{8,10},{10,12},{12,14},{14,16},{16,18},{18... | collective-permute-start | bytes 983048 | tf_op jit(solution)/shard_map/ppermute | solution.py:19
  32.6 3.0 %copy-start.4 = (f32[1,256,256]{2,1,0:T(8,128)S(1)}, f32[1,256,256]{2,1,0:T(8,128)}, u32[]{:S(2)}) copy-start(f32[1,256,256]{2,1,0:T(8,128)} %param.16) | copy-start | bytes 786436
  51.1 135.9 %reduce-scatter.2.cloned.1.call-start = ((), (), s32[]{:S(2)}) async-start(), calls=%async_computation.1 | async-start | bytes 2211840 | tf_op jit(solution)/shard_map/reduce_scatter | solution.py:130
  62.8 1.1 copy-start
  183.6 10.9 %copy-start.3 = (f32[2,256,256]{2,1,0:T(8,128)S(1)}, f32[2,256,256]{2,1,0:T(8,128)}, u32[]{:S(2)}) copy-start(f32[2,256,256]{2,1,0:T(8,128)} %get-tuple-element.71) | copy-start | bytes 1572868
  188.1 7.6 %collective-permute-start.2 = (f32[3,160,128]{2,1,0:T(8,128)S(1)}, f32[3,160,128]{2,1,0:T(8,128)S(1)}, u32[]{:S(2)}, u32[]{:S(2)}) collective-permute-start(f32[3,160,128]{2,1,0:T(8,128)S(1)} %get-tuple-element.81), channel_id=1, source_target_pairs={{0,2},{2,4},{4,6},{6,8},{8,10},{10,12},{12,14},{14,16},{16,18},{18... | collective-permute-start | bytes 737288 | tf_op jit(solution)/shard_map/ppermute | solution.py:19
  192.6 8.4 %collective-permute-start.3 = (f32[3,160,128]{2,1,0:T(8,128)S(1)}, f32[3,160,128]{2,1,0:T(8,128)S(1)}, u32[]{:S(2)}, u32[]{:S(2)}) collective-permute-start(f32[3,160,128]{2,1,0:T(8,128)S(1)} %get-tuple-element.82), channel_id=1, source_target_pairs={{2,0},{4,2},{6,4},{8,6},{10,8},{12,10},{14,12},{16,14},{18,16},{20... | collective-permute-start | bytes 737288 | tf_op jit(solution)/shard_map/ppermute | solution.py:20
  194.5 7.5 %copy-start.2 = (f32[2,160,128]{2,1,0:T(8,128)S(1)}, f32[2,160,128]{2,1,0:T(8,128)}, u32[]{:S(2)}) copy-start(f32[2,160,128]{2,1,0:T(8,128)} %param.14) | copy-start | bytes 491524
Sparse Core Ops, SparseCore 0:
  51.2 132.3 all-reduce.2
Sparse Core Ops, SparseCore 1:
  64.0 27.3 reduce-scatter.1
where the time goes:
time: 211 us; the launch traced here: 210 us
  waiting for transfers between devices  127 us (60%)
  matrix products  24.1 us (11%)
  between operations  19 us (9%)
  local copies, waits for them, and re-layouts  13.1 us (6%)
  starting transfers between devices  13 us (6%)
  other arithmetic  8.07 us (4%)
  blocking collectives  6.09 us (3%)
    psum x1, waiting for transfers between devices, local(): lax.psum((probe_grad, window_light), ('tile', 'group'))  119 us
    dot_general x8, matrix products, apply_right(): jnp.einsum('pjk,kl->pjl', values, matrix, precision=lax.Precision.HIGHEST)  12.3 us
    dot_general x8, matrix products, apply_left(): jnp.einsum('jk,pkl->pjl', matrix, values, precision=lax.Precision.HIGHEST)  11.8 us
    dynamic_update_slice x1, local copies, waits for them, and re-layouts, place(): return lax.dynamic_update_slice(current, piece + terms[slot], corner)  10.7 us
    ppermute x2, starting transfers between devices, padded_2(): before = lax.ppermute(last, axis, up)  7.55 us
    ppermute x2, waiting for transfers between devices, padded_2(): after = lax.ppermute(initial, axis, down)  6.25 us
    all_gather x1, blocking collectives, local(): full_rows = lax.all_gather(object_field, 'group', axis=1, tiled=True)  6.09 us
    ppermute x2, starting transfers between devices, padded_2(): after = lax.ppermute(initial, axis, down)  5.35 us
  transfers between devices with their start and end apart: 6, of which 5 were waited for; matrix products, arithmetic and copies ran while one was open for 7% of the time, Pallas kernels for 0%

commit v1 on v0

v1 whole, which is shorter than its diff:
```python
import functools
import math

import jax
import jax.numpy as jnp
import numpy as np
from jax import lax
from jax.experimental import pallas as pl
from jax.experimental.pallas import tpu as pltpu
from jax.sharding import PartitionSpec as P

MESH = pl.DeviceIdType.MESH
F32 = jnp.float32
BF16 = jnp.bfloat16


def dft_tables(length):
    k = np.arange(length)
    angles = 2.0 * math.pi / length * (np.outer(k, k) % length)
    cos, sin = np.cos(angles) / math.sqrt(length), np.sin(angles) / math.sqrt(length)
    full = np.block([[cos, sin], [-sin, cos]]).astype(np.float32)
    head = full.astype(BF16)
    tail = (full - head.astype(np.float32)).astype(BF16)
    return head, tail


def split(x):
    head = x.astype(BF16)
    return head, (x - head.astype(F32)).astype(BF16)


def mm(a, b):
    return jnp.dot(a, b, preferred_element_type=F32)


def table_left(head, tail, x):
    xh, xl = split(x)
    return mm(head, xh) + (mm(head, xl) + mm(tail, xh))


def table_right(x, head, tail):
    xh, xl = split(x)
    return mm(xh, head) + (mm(xl, head) + mm(xh, tail))


def remote(src, dst, send, recv, tile, group):
    return pltpu.make_async_remote_copy(
        src_ref=src, dst_ref=dst, send_sem=send, recv_sem=recv,
        device_id={"tile": tile, "group": group}, device_id_type=MESH,
    )


class AllReduce:
    def __init__(self, plan, part, pair, mine, came, full, sems):
        self.p, self.part, self.pair, self.mine = plan, part, pair, mine
        self.came, self.full, self.sems = came, full, sems

    def pair_copy(self):
        p = self.p
        return remote(self.part.at[1 - p.h, p.s], self.pair, self.sems[0].at[0],
                      self.sems[1].at[0], p.partner, p.g)

    def spread_copy(self, d):
        p = self.p
        to = lax.rem(p.k + d, p.H)
        return remote(self.mine.at[to], self.came.at[d - 1], self.sems[2].at[d - 1],
                      self.sems[3].at[d - 1], 2 * to + p.h, p.g)

    def collect_copy(self, dg, dk, arriving):
        p = self.p
        n = dg * p.H + dk
        sign = -1 if arriving else 1
        k = lax.rem(p.k + sign * dk + p.H, p.H)
        s = lax.rem(p.s + sign * dg + p.gs, p.gs)
        slot = self.full.at[p.h, s, k] if arriving else self.full.at[p.h, p.s, p.k]
        return remote(slot, slot, self.sems[4].at[n], self.sems[5].at[n],
                      2 * k + p.h, p.g - p.s + s)

    def relay_copy(self, dg, dk, arriving):
        p = self.p
        n = dg * p.H + dk
        k = lax.rem(p.k - dk + p.H, p.H)
        s = lax.rem(p.s - dg + p.gs, p.gs)
        h = 1 - p.h if arriving else p.h
        slot = self.full.at[h, s, k]
        return remote(slot, slot, self.sems[6].at[n], self.sems[7].at[n], p.partner, p.g)

    def others(self):
        p = self.p
        return [(dg, dk) for dk in range(p.H) for dg in range(p.gs) if dg or dk]

    def put(self, channel, value):
        p = self.p
        self.part[:, :, :, channel] = value.reshape(2, p.gs, p.H, p.rows, value.shape[-1])

    def start_pair(self):
        self.pair_copy().start()

    def start_spread(self):
        p = self.p
        self.pair_copy().wait()
        self.mine[...] = self.part[p.h, p.s] + self.pair[...]
        for d in range(1, p.H):
            self.spread_copy(d).start()

    def start_collect(self):
        p = self.p
        total = self.mine[p.k]
        for d in range(1, p.H):
            self.spread_copy(d).wait()
            total = total + self.came[d - 1]
        self.full[p.h, p.s, p.k] = total
        for dg, dk in self.others():
            self.collect_copy(dg, dk, False).start()
        self.relay_copy(0, 0, False).start()

    def relay(self):
        for dg, dk in self.others():
            self.collect_copy(dg, dk, True).wait_recv()
            self.relay_copy(dg, dk, False).start()

    def finish(self):
        self.relay_copy(0, 0, True).wait_recv()
        self.relay_copy(0, 0, False).wait_send()
        for dg, dk in self.others():
            self.relay_copy(dg, dk, True).wait_recv()
            self.relay_copy(dg, dk, False).wait_send()
            self.collect_copy(dg, dk, False).wait_send()

    def get(self, channel):
        whole = self.full[:, :, :, channel]
        return whole.reshape(-1, whole.shape[-1])


class Plan:
    pass


def kernel(T, G, gs, obj, probe, amp, scal_in, a_head, a_tail, b_head, b_tail,
           new_obj, new_probe, pad, amps, scal, win, terms, light_terms, acc, acc_light,
           edge, edge_light, grad_sum, *rest):
    t, g = lax.axis_index("tile"), lax.axis_index("group")
    R, W = obj.shape[1], probe.shape[1]
    B = obj.shape[2]
    rows = pad.shape[2]
    p = Plan()
    p.g, p.H, p.gs = g, T // 2, gs
    p.k, p.h = lax.div(t, 2), lax.rem(t, 2)
    p.partner = t + 1 - 2 * p.h
    p.s = lax.rem(g, gs)
    p.rows = W // 2 // (p.H * gs)
    light_red = AllReduce(p, *rest[0:5], rest[5:13])
    grad_red = AllReduce(p, *rest[13:18], rest[18:26])
    (own_s, own_r, side_s, side_r, amp_s, amp_r, scal_s, scal_r,
     edge_s, edge_r) = rest[26:36]

    barrier = pltpu.get_barrier_semaphore()
    count = 0
    for dt in range(T):
        for dg in range(G):
            same_block = G == gs
            if (dt or dg) and (same_block or dt == 0 or dg == 0):
                pl.semaphore_signal(
                    barrier, inc=1,
                    device_id={"tile": lax.rem(t + dt, T), "group": lax.rem(g + dg, G)},
                    device_id_type=MESH)
                count += 1
    pl.semaphore_wait(barrier, count)

    def span(group):
        return pl.ds(pl.multiple_of(group * R, 8), R)

    def to_peer(j, arriving):
        peer = lax.rem(g + (G - j if arriving else j), G)
        slot = pad.at[1, :, span(peer if arriving else g)]
        return remote(slot if arriving else obj, slot, own_s.at[j - 1], own_r.at[j - 1], t, peer)

    def to_side(j, right, arriving):
        who = lax.rem(g + G - j, G)
        block = (0 if right else 2)
        dst = pad.at[block, :, span(who)]
        src = obj if j == 0 else pad.at[1, :, span(who)]
        n = 2 * j + int(right)
        return remote(dst if arriving else src, dst, side_s.at[n], side_r.at[n],
                      (t + 1 if right else t - 1) if not arriving else (t - 1 if right else t + 1), g)

    def amp_copy(j, arriving):
        peer = lax.rem(g + (G - j if arriving else j), G)
        slot = amps.at[peer if arriving else g]
        return remote(slot if arriving else amp.at[0], slot, amp_s.at[j - 1], amp_r.at[j - 1], t, peer)

    def scal_copy(j, arriving):
        peer = lax.rem(g + (G - j if arriving else j), G)
        slot = scal.at[peer if arriving else g]
        return remote(slot if arriving else scal_in, slot, scal_s.at[j - 1], scal_r.at[j - 1], t, peer)

    def edge_copy(src, dst, right, base, arriving):
        n = base + int(right)
        side = dst.at[0 if right else 1]
        if arriving:
            return remote(side, side, edge_s.at[n], edge_r.at[n], t - 1 if right else t + 1, g)
        return remote(src.at[2 if right else 0], side, edge_s.at[n], edge_r.at[n],
                      t + 1 if right else t - 1, g)

    not_first, not_last = t > 0, t < T - 1

    for j in range(1, G):
        to_peer(j, False).start()
    pl.when(not_first)(lambda: to_side(0, False, False).start())
    pl.when(not_last)(lambda: to_side(0, True, False).start())
    for j in range(1, G):
        scal_copy(j, False).start()
    for j in range(1, G):
        amp_copy(j, False).start()

    pad[1, :, span(g)] = obj[...]
    scal[g] = scal_in[...]
    amps[g] = amp[0]

    @pl.when(t == 0)
    def _():
        pad[0] = jnp.zeros(pad.shape[1:], F32)
        edge[0] = jnp.zeros(edge.shape[1:], F32)
        edge_light[0] = jnp.zeros(edge_light.shape[1:], F32)

    @pl.when(t == T - 1)
    def _():
        pad[2] = jnp.zeros(pad.shape[1:], F32)
        edge[1] = jnp.zeros(edge.shape[1:], F32)
        edge_light[1] = jnp.zeros(edge_light.shape[1:], F32)

    spare = rows - W
    blocks = W // B
    terms[:, :, 0:spare] = jnp.zeros((2, blocks, spare, B), F32)
    terms[:, :, spare + W:] = jnp.zeros((2, blocks, spare, B), F32)
    light_terms[:, 0:spare] = jnp.zeros((blocks, spare, B), F32)
    light_terms[:, spare + W:] = jnp.zeros((blocks, spare, B), F32)

    def hold(ref, value):
        for b in range(blocks):
            ref[b, spare:spare + W] = value[:, b * B:(b + 1) * B]

    probe_light = probe[0] * probe[0] + probe[1] * probe[1]
    hold(light_terms, probe_light)
    light_max = jnp.max(probe_light) + 1e-06

    for j in range(1, G):
        to_peer(j, True).wait_recv()
        pl.when(not_first)(lambda: to_side(j, False, False).start())
        pl.when(not_last)(lambda: to_side(j, True, False).start())
    for j in range(1, G):
        scal_copy(j, True).wait_recv()
    for j in range(G):
        pl.when(not_last)(lambda: to_side(j, False, True).wait_recv())
        pl.when(not_first)(lambda: to_side(j, True, True).wait_recv())

    def numbers(k):
        return scal[k, 0, 0], scal[k, 1, 0], scal[k, 2, 0].astype(F32)

    def placed(ref, row, column):
        first = g * R + spare - row
        pieces = [ref[b, pl.ds(first, R), :] for b in range(blocks)]
        wide = jnp.concatenate(pieces + [jnp.zeros((R, 3 * B - W), F32)], axis=1)
        return pltpu.roll(wide, column, 1)

    acc[...] = jnp.zeros(acc.shape, F32)
    acc_light[...] = jnp.zeros(acc_light.shape, F32)
    grad_sum[...] = jnp.zeros(grad_sum.shape, F32)

    def look(j, light):
        k = lax.rem(g + j, G)
        row, column, weight = numbers(k)
        for ch in range(2):
            wide = jnp.concatenate([pad[b, ch, pl.ds(row, W), :] for b in range(3)], axis=1)
            win[k, ch] = pltpu.roll(wide, lax.rem(3 * B - column, 3 * B), 1)[:, 0:W]
        spread = weight * placed(light_terms, row, column)
        for b in range(3):
            acc_light[b] += spread[:, b * B:(b + 1) * B]
        return light + weight * (win[k, 0] * win[k, 0] + win[k, 1] * win[k, 1])

    light = lax.fori_loop(0, G, look, jnp.zeros((W, W), F32))
    light_red.put(0, light)
    light_red.start_pair()
    pl.when(not_first)(lambda: edge_copy(acc_light, edge_light, False, 0, False).start())
    pl.when(not_last)(lambda: edge_copy(acc_light, edge_light, True, 0, False).start())

    def position(k):
        row, column, weight = numbers(k)
        wr, wi = win[k, 0], win[k, 1]
        pr, pi = probe[0], probe[1]
        x = jnp.concatenate([pr * wr - pi * wi, pr * wi + pi * wr], axis=0)
        y = table_left(a_head[...], a_tail[...], x)
        z = table_right(jnp.concatenate([y[:W], y[W:]], axis=1), b_head[...], b_tail[...])
        zr, zi = z[:, :W], z[:, W:]
        factor = 1.0 - amps[k] * lax.rsqrt(jnp.maximum(zr * zr + zi * zi, 0.0625))
        x = jnp.concatenate([zr * factor, zi * factor], axis=0)
        y = table_left(b_head[...], b_tail[...], x)
        z = table_right(jnp.concatenate([y[:W], y[W:]], axis=1), a_head[...], a_tail[...])
        mr, mi = z[:, :W] * weight, z[:, W:] * weight
        hold(terms.at[0], pr * mr + pi * mi)
        hold(terms.at[1], pr * mi - pi * mr)
        grad_sum[0] += wr * mr + wi * mi
        grad_sum[1] += wr * mi - wi * mr
        for ch in range(2):
            spread = placed(terms.at[ch], row, column)
            for b in range(3):
                acc[b, ch] += spread[:, b * B:(b + 1) * B]

    position(g)
    light_red.start_spread()
    for j in range(1, G):
        amp_copy(j, True).wait_recv()
    pl.loop(1, G)(lambda j: position(lax.rem(g + j, G)))

    for ch in range(2):
        grad_red.put(ch, grad_sum[ch])
    grad_red.start_pair()
    light_red.start_collect()
    grad_red.start_spread()
    pl.when(not_first)(lambda: edge_copy(acc, edge, False, 2, False).start())
    pl.when(not_last)(lambda: edge_copy(acc, edge, True, 2, False).start())
    light_red.relay()
    grad_red.start_collect()

    for src, dst, base in ((acc_light, edge_light, 0), (acc, edge, 2)):
        pl.when(not_last)(lambda: edge_copy(src, dst, False, base, True).wait_recv())
        pl.when(not_first)(lambda: edge_copy(src, dst, True, base, True).wait_recv())
    below = 1.0 / (acc_light[1] + edge_light[0] + edge_light[1] + 0.25 * light_max)
    for ch in range(2):
        new_obj[ch] = obj[ch] - (acc[1, ch] + edge[0, ch] + edge[1, ch]) * below
    light_red.finish()
    light = light_red.get(0)
    below = 1.0 / (light + 0.25 * jnp.mean(light) + 1e-05)
    grad_red.relay()
    grad_red.finish()
    for ch in range(2):
        new_probe[ch] = probe[ch] - grad_red.get(ch) * below

    for j in range(1, G):
        to_peer(j, False).wait_send()
        amp_copy(j, False).wait_send()
        scal_copy(j, False).wait_send()
    for j in range(G):
        pl.when(not_first)(lambda: to_side(j, False, False).wait_send())
        pl.when(not_last)(lambda: to_side(j, True, False).wait_send())
    for src, dst, base in ((acc_light, edge_light, 0), (acc, edge, 2)):
        pl.when(not_first)(lambda: edge_copy(src, dst, False, base, False).wait_send())
        pl.when(not_last)(lambda: edge_copy(src, dst, True, base, False).wait_send())


def local(T, G, object_field, probe_field, amplitudes, row_start, column_start, live_slots):
    R, B = object_field.shape[1:]
    W = probe_field.shape[1]
    rows = R * G
    H = T // 2
    gs = max(n for n in range(1, G + 1) if G % n == 0 and n * H * 8 <= W // 2)
    chunk = W // 2 // (H * gs)
    head, tail = dft_tables(W)
    scal = jnp.concatenate([row_start, column_start, live_slots, live_slots]).astype(jnp.int32)
    scal = jnp.broadcast_to(jnp.concatenate([scal, scal])[:, None], (8, 128))
    spare = rows - W
    dma = lambda n: pltpu.SemaphoreType.DMA((max(n, 1),))

    def reduce_scratch(channels):
        return [
            pltpu.VMEM((2, gs, H, channels, chunk, W), F32),
            pltpu.VMEM((H, channels, chunk, W), F32),
            pltpu.VMEM((H, channels, chunk, W), F32),
            pltpu.VMEM((H - 1, channels, chunk, W), F32),
            pltpu.VMEM((2, gs, H, channels, chunk, W), F32),
            dma(1), dma(1), dma(H - 1), dma(H - 1), dma(gs * H), dma(gs * H), dma(gs * H), dma(gs * H),
        ]

    vmem = pl.BlockSpec(memory_space=pltpu.VMEM)
    return pl.pallas_call(
        functools.partial(kernel, T, G, gs),
        out_shape=(jax.ShapeDtypeStruct(object_field.shape, F32),
                   jax.ShapeDtypeStruct(probe_field.shape, F32)),
        in_specs=[vmem] * 8,
        out_specs=(vmem, vmem),
        scratch_shapes=[
            pltpu.VMEM((3, 2, rows, B), F32),
            pltpu.VMEM((G, W, W), F32),
            pltpu.VMEM((G, 8, 128), jnp.int32),
            pltpu.VMEM((G, 2, W, W), F32),
            pltpu.VMEM((2, W // B, W + 2 * spare, B), F32),
            pltpu.VMEM((W // B, W + 2 * spare, B), F32),
            pltpu.VMEM((3, 2, R, B), F32),
            pltpu.VMEM((3, R, B), F32),
            pltpu.VMEM((2, 2, R, B), F32),
            pltpu.VMEM((2, R, B), F32),
            pltpu.VMEM((2, W, W), F32),
            *reduce_scratch(1),
            *reduce_scratch(2),
            dma(G - 1), dma(G - 1), dma(2 * G), dma(2 * G), dma(G - 1), dma(G - 1),
            dma(G - 1), dma(G - 1), dma(4), dma(4),
        ],
        compiler_params=pltpu.CompilerParams(
            collective_id=0, has_side_effects=True, vmem_limit_bytes=60 * 1024 * 1024),
    )(object_field, probe_field, amplitudes, scal, head, tail, head.T, tail.T)


def solution(mesh):
    return jax.shard_map(
        functools.partial(local, mesh.shape["tile"], mesh.shape["group"]),
        mesh=mesh,
        in_specs=(
            P(None, "group", "tile"),
            P(),
            P(("tile", "group"), None, None),
            P(("tile", "group")),
            P(("tile", "group")),
            P(("tile", "group")),
        ),
        out_specs=(P(None, "group", "tile"), P()),
        check_vma=False,
    )
```

time: 211 us -> 51.8 us (0.25)
  the two profiles are of different devices: /device:TPU:3 before, /device:TPU:0 now
where the time goes in v1:
time: 51.8 us; the launch traced here: 51.5 us
  Pallas kernels  44.7 us (86%)
  local copies, waits for them, and re-layouts  4.21 us (8%)
  between operations  2.58 us (5%)
    pallas_call x1, Pallas kernels, local(): pl.pallas_call(functools.partial(kernel, T, G, gs), out_shape=(jax.ShapeD...  44.7 us
    unnamed x2, local copies, waits for them, and re-layouts  3.46 us

profile of v1, /device:TPU:0, one launch (start us, length us, event | category | flops | bytes accessed | tf_op | source)
XLA Modules:
  0.0 51.5 jit_solution(908849037690884819)
XLA Ops:
  2.6 0.1 concatenate.5
  2.7 0.7 %broadcast_in_dim.2.scal_in = s32[8,128]{1,0:T(8,128)} broadcast(s32[8]{0:T(128)S(1)} %concatenate.5), dimensions={0} | broadcast | bytes 4128 | tf_op jit(solution)/shard_map/broadcast_in_dim | solution.py:360
  3.3 44.7 %shard_map.113 = (f32[2,160,128]{2,1,0:T(8,128)}, f32[2,256,256]{2,1,0:T(8,128)}) custom-call(f32[2,160,128]{2,1,0:T(8,128)} %obj.1, f32[2,256,256]{2,1,0:T(8,128)} %probe.1, f32[1,256,256]{2,1,0:T(8,128)} %amp.1, s32[8,128]{1,0:T(8,128)} %broadcast_in_dim.2.scal_in, bf16[512,512]{1,0:T(8,128)(2,1)} %constant.8.clone.a_head, ...), custom_call_target="tpu_custom_call" | custom-call | tf_op jit(solution)/shard_map/pallas_call | solution.py:375
  48.0 1.6 %copy.17 = f32[2,160,128]{2,1,0:T(8,128)} copy(f32[2,160,128]{2,1,0:T(8,128)} %get-tuple-element.4) | data formatting | bytes 327680
  49.6 1.9 %copy.18 = f32[2,256,256]{2,1,0:T(8,128)} copy(f32[2,256,256]{2,1,0:T(8,128)} %get-tuple-element.5) | data formatting | bytes 1048576

commit v2 on v1

--- a/solution.py
+++ b/solution.py
@@ -136,10 +136,20 @@
     pass
 
 
-def kernel(T, G, gs, obj, probe, amp, scal_in, a_head, a_tail, b_head, b_tail,
-           new_obj, new_probe, pad, amps, scal, win, terms, light_terms, acc, acc_light,
+def kernel(T, G, gs, row_in, column_in, live_in, obj, probe_in, amp, *args):
+    tables_in, args = args[:4], args[4:]
+    (obj_step, probe_step, scal_in, probe, *args) = args
+    (a_head, a_tail, b_head, b_tail, load_sem, far), args = args[:6], args[6:]
+    body(T, G, gs, (row_in, column_in, live_in), (obj, probe_in, amp, *tables_in),
+         (probe, a_head, a_tail, b_head, b_tail), load_sem, far, scal_in, probe, a_head, a_tail,
+         b_head, b_tail, obj_step, probe_step, *args)
+
+
+def body(T, G, gs, scalars, inputs, loaded, load_sem, far, scal_in, probe, a_head, a_tail, b_head,
+         b_tail, obj_step, probe_step, pad, amps, scal_all, win, terms, light_terms, acc, acc_light,
            edge, edge_light, grad_sum, *rest):
     t, g = lax.axis_index("tile"), lax.axis_index("group")
+    obj, probe_in, amp, *tables_in = inputs
     R, W = obj.shape[1], probe.shape[1]
     B = obj.shape[2]
     rows = pad.shape[2]
@@ -154,40 +164,55 @@
     (own_s, own_r, side_s, side_r, amp_s, amp_r, scal_s, scal_r,
      edge_s, edge_r) = rest[26:36]
 
+    own = pad.at[1, :, pl.ds(pl.multiple_of(g * R, 8), R)]
+    loads = [pltpu.make_async_copy(src, dst, load_sem.at[i]) for i, (src, dst) in enumerate(
+        [(obj, own), (amp.at[0], amps.at[g]), *zip((probe_in, *tables_in), loaded)])]
+    for load in loads:
+        load.start()
     barrier = pltpu.get_barrier_semaphore()
     count = 0
     for dt in range(T):
         for dg in range(G):
-            same_block = G == gs
-            if (dt or dg) and (same_block or dt == 0 or dg == 0):
+            if (dt or dg) and (dt == 0 or (dt % 2 == 0 and (G == gs or dg == 0))):
                 pl.semaphore_signal(
                     barrier, inc=1,
                     device_id={"tile": lax.rem(t + dt, T), "group": lax.rem(g + dg, G)},
                     device_id_type=MESH)
                 count += 1
-    pl.semaphore_wait(barrier, count)
+    for to, there in ((t - 1, t > 0), (t + 1, t < T - 1)):
+        @pl.when(there)
+        def _():
+            pl.semaphore_signal(barrier, inc=1, device_id={"tile": to, "group": g}, device_id_type=MESH)
+    scal = scal_all
+    line = lax.broadcasted_iota(jnp.int32, scal_in.shape, 0)
+    scal_in[...] = jnp.where(line == 0, scalars[0][0], jnp.where(line == 1, scalars[1][0], scalars[2][0]))
+    edges_here = (t > 0).astype(jnp.int32) + (t < T - 1).astype(jnp.int32)
+    pl.semaphore_wait(barrier, count + edges_here)
+    loads[0].wait()
+    loads[1].wait()
 
     def span(group):
         return pl.ds(pl.multiple_of(group * R, 8), R)
 
-    def to_peer(j, arriving):
+    def to_peer(j, ch, arriving):
         peer = lax.rem(g + (G - j if arriving else j), G)
-        slot = pad.at[1, :, span(peer if arriving else g)]
-        return remote(slot if arriving else obj, slot, own_s.at[j - 1], own_r.at[j - 1], t, peer)
-
-    def to_side(j, right, arriving):
+        slot = pad.at[1, ch, span(peer if arriving else g)]
+        n = 2 * (j - 1) + ch
+        return remote(slot, slot, own_s.at[n], own_r.at[n], t, peer)
+
+    def to_side(j, ch, right, arriving):
         who = lax.rem(g + G - j, G)
         block = (0 if right else 2)
-        dst = pad.at[block, :, span(who)]
-        src = obj if j == 0 else pad.at[1, :, span(who)]
-        n = 2 * j + int(right)
+        dst = pad.at[block, ch, span(who)]
+        src = pad.at[1, ch, span(who)]
+        n = 4 * j + 2 * ch + int(right)
         return remote(dst if arriving else src, dst, side_s.at[n], side_r.at[n],
                       (t + 1 if right else t - 1) if not arriving else (t - 1 if right else t + 1), g)
 
     def amp_copy(j, arriving):
         peer = lax.rem(g + (G - j if arriving else j), G)
         slot = amps.at[peer if arriving else g]
-        return remote(slot if arriving else amp.at[0], slot, amp_s.at[j - 1], amp_r.at[j - 1], t, peer)
+        return remote(slot, slot, amp_s.at[j - 1], amp_r.at[j - 1], t, peer)
 
     def scal_copy(j, arriving):
         peer = lax.rem(g + (G - j if arriving else j), G)
@@ -204,18 +229,18 @@
 
     not_first, not_last = t > 0, t < T - 1
 
-    for j in range(1, G):
-        to_peer(j, False).start()
-    pl.when(not_first)(lambda: to_side(0, False, False).start())
-    pl.when(not_last)(lambda: to_side(0, True, False).start())
+    for ch in range(2):
+        for j in range(1, G):
+            to_peer(j, ch, False).start()
+    for ch in range(2):
+        pl.when(not_first)(lambda: to_side(0, ch, False, False).start())
+        pl.when(not_last)(lambda: to_side(0, ch, True, False).start())
     for j in range(1, G):
         scal_copy(j, False).start()
     for j in range(1, G):
         amp_copy(j, False).start()
 
-    pad[1, :, span(g)] = obj[...]
     scal[g] = scal_in[...]
-    amps[g] = amp[0]
 
     @pl.when(t == 0)
     def _():
@@ -240,19 +265,23 @@
         for b in range(blocks):
             ref[b, spare:spare + W] = value[:, b * B:(b + 1) * B]
 
+    for load in loads[2:]:
+        load.wait()
     probe_light = probe[0] * probe[0] + probe[1] * probe[1]
     hold(light_terms, probe_light)
     light_max = jnp.max(probe_light) + 1e-06
 
-    for j in range(1, G):
-        to_peer(j, True).wait_recv()
-        pl.when(not_first)(lambda: to_side(j, False, False).start())
-        pl.when(not_last)(lambda: to_side(j, True, False).start())
+    for ch in range(2):
+        for j in range(1, G):
+            to_peer(j, ch, True).wait_recv()
+            pl.when(not_first)(lambda: to_side(j, ch, False, False).start())
+            pl.when(not_last)(lambda: to_side(j, ch, True, False).start())
     for j in range(1, G):
         scal_copy(j, True).wait_recv()
     for j in range(G):
-        pl.when(not_last)(lambda: to_side(j, False, True).wait_recv())
-        pl.when(not_first)(lambda: to_side(j, True, True).wait_recv())
+        for ch in range(2):
+            pl.when(not_last)(lambda: to_side(j, ch, False, True).wait_recv())
+            pl.when(not_first)(lambda: to_side(j, ch, True, True).wait_recv())
 
     def numbers(k):
         return scal[k, 0, 0], scal[k, 1, 0], scal[k, 2, 0].astype(F32)
@@ -284,8 +313,7 @@
     pl.when(not_first)(lambda: edge_copy(acc_light, edge_light, False, 0, False).start())
     pl.when(not_last)(lambda: edge_copy(acc_light, edge_light, True, 0, False).start())
 
-    def position(k):
-        row, column, weight = numbers(k)
+    def forth(k):
         wr, wi = win[k, 0], win[k, 1]
         pr, pi = probe[0], probe[1]
         x = jnp.concatenate([pr * wr - pi * wi, pr * wi + pi * wr], axis=0)
@@ -293,7 +321,13 @@
         z = table_right(jnp.concatenate([y[:W], y[W:]], axis=1), b_head[...], b_tail[...])
         zr, zi = z[:, :W], z[:, W:]
         factor = 1.0 - amps[k] * lax.rsqrt(jnp.maximum(zr * zr + zi * zi, 0.0625))
-        x = jnp.concatenate([zr * factor, zi * factor], axis=0)
+        far[0:W], far[W:] = zr * factor, zi * factor
+
+    def back(k):
+        row, column, weight = numbers(k)
+        wr, wi = win[k, 0], win[k, 1]
+        pr, pi = probe[0], probe[1]
+        x = far[...]
         y = table_left(b_head[...], b_tail[...], x)
         z = table_right(jnp.concatenate([y[:W], y[W:]], axis=1), a_head[...], a_tail[...])
         mr, mi = z[:, :W] * weight, z[:, W:] * weight
@@ -306,19 +340,30 @@
             for b in range(3):
                 acc[b, ch] += spread[:, b * B:(b + 1) * B]
 
-    position(g)
+    forth(g)
     light_red.start_spread()
+    back(g)
     for j in range(1, G):
         amp_copy(j, True).wait_recv()
-    pl.loop(1, G)(lambda j: position(lax.rem(g + j, G)))
+
+    def both(j):
+        back(lax.rem(g + j, G))
+        forth(lax.rem(g + j + 1, G))
+
+    if G > 1:
+        forth(lax.rem(g + 1, G))
+        light_red.start_collect()
+        pl.loop(1, G - 1)(both)
+        back(lax.rem(g + G - 1, G))
+    else:
+        light_red.start_collect()
 
     for ch in range(2):
         grad_red.put(ch, grad_sum[ch])
     grad_red.start_pair()
-    light_red.start_collect()
-    grad_red.start_spread()
     pl.when(not_first)(lambda: edge_copy(acc, edge, False, 2, False).start())
     pl.when(not_last)(lambda: edge_copy(acc, edge, True, 2, False).start())
+    grad_red.start_spread()
     light_red.relay()
     grad_red.start_collect()
 
@@ -327,22 +372,24 @@
         pl.when(not_first)(lambda: edge_copy(src, dst, True, base, True).wait_recv())
     below = 1.0 / (acc_light[1] + edge_light[0] + edge_light[1] + 0.25 * light_max)
     for ch in range(2):
-        new_obj[ch] = obj[ch] - (acc[1, ch] + edge[0, ch] + edge[1, ch]) * below
+        obj_step[ch] = (acc[1, ch] + edge[0, ch] + edge[1, ch]) * below
     light_red.finish()
     light = light_red.get(0)
     below = 1.0 / (light + 0.25 * jnp.mean(light) + 1e-05)
     grad_red.relay()
     grad_red.finish()
     for ch in range(2):
-        new_probe[ch] = probe[ch] - grad_red.get(ch) * below
+        probe_step[ch] = grad_red.get(ch) * below
 
     for j in range(1, G):
-        to_peer(j, False).wait_send()
+        for ch in range(2):
+            to_peer(j, ch, False).wait_send()
         amp_copy(j, False).wait_send()
         scal_copy(j, False).wait_send()
     for j in range(G):
-        pl.when(not_first)(lambda: to_side(j, False, False).wait_send())
-        pl.when(not_last)(lambda: to_side(j, True, False).wait_send())
+        for ch in range(2):
+            pl.when(not_first)(lambda: to_side(j, ch, False, False).wait_send())
+            pl.when(not_last)(lambda: to_side(j, ch, True, False).wait_send())
     for src, dst, base in ((acc_light, edge_light, 0), (acc, edge, 2)):
         pl.when(not_first)(lambda: edge_copy(src, dst, False, base, False).wait_send())
         pl.when(not_last)(lambda: edge_copy(src, dst, True, base, False).wait_send())
@@ -356,8 +403,6 @@
     gs = max(n for n in range(1, G + 1) if G % n == 0 and n * H * 8 <= W // 2)
     chunk = W // 2 // (H * gs)
     head, tail = dft_tables(W)
-    scal = jnp.concatenate([row_start, column_start, live_slots, live_slots]).astype(jnp.int32)
-    scal = jnp.broadcast_to(jnp.concatenate([scal, scal])[:, None], (8, 128))
     spare = rows - W
     dma = lambda n: pltpu.SemaphoreType.DMA((max(n, 1),))
 
@@ -371,14 +416,21 @@
             dma(1), dma(1), dma(H - 1), dma(H - 1), dma(gs * H), dma(gs * H), dma(gs * H), dma(gs * H),
         ]
 
+    vmem_limit = 67043328 - 4 * (object_field.size + probe_field.size) - 65536
+    smem = pl.BlockSpec(memory_space=pltpu.SMEM)
+    hbm = pl.BlockSpec(memory_space=pltpu.HBM)
     vmem = pl.BlockSpec(memory_space=pltpu.VMEM)
-    return pl.pallas_call(
+    obj_step, probe_step = pl.pallas_call(
         functools.partial(kernel, T, G, gs),
-        out_shape=(jax.ShapeDtypeStruct(object_field.shape, F32),
-                   jax.ShapeDtypeStruct(probe_field.shape, F32)),
-        in_specs=[vmem] * 8,
+        out_shape=(pltpu.VMEM(object_field.shape, F32), pltpu.VMEM(probe_field.shape, F32)),
+        in_specs=[smem] * 3 + [hbm] * 7,
         out_specs=(vmem, vmem),
         scratch_shapes=[
+            pltpu.VMEM((8, 128), jnp.int32),
+            pltpu.VMEM(probe_field.shape, F32),
+            *[pltpu.VMEM(head.shape, BF16)] * 4,
+            dma(7),
+            pltpu.VMEM((2 * W, W), F32),
             pltpu.VMEM((3, 2, rows, B), F32),
             pltpu.VMEM((G, W, W), F32),
             pltpu.VMEM((G, 8, 128), jnp.int32),
@@ -392,12 +444,14 @@
             pltpu.VMEM((2, W, W), F32),
             *reduce_scratch(1),
             *reduce_scratch(2),
-            dma(G - 1), dma(G - 1), dma(2 * G), dma(2 * G), dma(G - 1), dma(G - 1),
+            dma(2 * G - 2), dma(2 * G - 2), dma(4 * G), dma(4 * G), dma(G - 1), dma(G - 1),
             dma(G - 1), dma(G - 1), dma(4), dma(4),
         ],
         compiler_params=pltpu.CompilerParams(
-            collective_id=0, has_side_effects=True, vmem_limit_bytes=60 * 1024 * 1024),
-    )(object_field, probe_field, amplitudes, scal, head, tail, head.T, tail.T)
+            collective_id=0, has_side_effects=True, vmem_limit_bytes=vmem_limit),
+    )(row_start, column_start, live_slots, object_field, probe_field, amplitudes, head, tail,
+      head.T, tail.T)
+    return object_field - obj_step, probe_field - probe_step
 
 
 def solution(mesh):

time: 51.8 us -> 48 us (0.927)
  local copies, waits for them, and re-layouts: 4.21 us -> 0 us
  other arithmetic: 0 us -> 3.5 us
  Pallas kernels: 44.7 us -> 41.7 us
    sub x0 -> x2, other arithmetic: none -> 3.5 us  [local(): return (object_field - obj_step, probe_field - probe_step)]
    unnamed x2 -> x0, local copies, waits for them, and re-layouts: 3.46 us -> none
    pallas_call x1, Pallas kernels: 44.7 us -> 41.7 us  [local(): pl.pallas_call(functools.partial(kernel, T, G, gs), out_shape=(pltpu.VMEM...]
    broadcast_in_dim x1 -> x0, local copies, waits for them, and re-layouts: 0.67 us -> none  [local(): scal = jnp.broadcast_to(jnp.concatenate([scal, scal])[:, None], (8, 128))]
where the time goes in v2:
time: 48 us; the launch traced here: 47.7 us
  Pallas kernels  41.7 us (87%)
  other arithmetic  3.5 us (7%)
  between operations  2.58 us (5%)
    pallas_call x1, Pallas kernels, local(): pl.pallas_call(functools.partial(kernel, T, G, gs), out_shape=(pltpu.VMEM...  41.7 us
    sub x2, other arithmetic, local(): return (object_field - obj_step, probe_field - probe_step)  3.5 us

profile of v2, /device:TPU:0, one launch (start us, length us, event | category | flops | bytes accessed | tf_op | source)
XLA Modules:
  0.0 47.7 jit_solution(820016985340329388)
XLA Ops:
  2.6 41.7 %shard_map.113 = (f32[2,160,128]{2,1,0:T(8,128)S(1)}, f32[2,256,256]{2,1,0:T(8,128)S(1)}) custom-call(s32[1]{0:T(128)S(6)} %copy.12.row_in, s32[1]{0:T(128)S(6)} %copy.13.column_in, s32[1]{0:T(128)S(6)} %copy.14.live_in, f32[2,160,128]{2,1,0:T(8,128)} %obj.1, f32[2,256,256]{2,1,0:T(8,128)} %probe_in.1, f32[1,256,256]{2,1,0:T(8,128)} %amp.1, ...), custom_call_target="tpu_custom_call" | custom-call | tf_op jit(solution)/shard_map/pallas_call | solution.py:423
  44.2 1.6 %sub.6 = f32[2,160,128]{2,1,0:T(8,128)} subtract(f32[2,160,128]{2,1,0:T(8,128)} %obj.1, f32[2,160,128]{2,1,0:T(8,128)S(1)} %get-tuple-element.4) | non-fusion elementwise | flops 40960 | bytes 491520 | tf_op jit(solution)/shard_map/sub | solution.py:454
  45.8 1.9 %sub.7 = f32[2,256,256]{2,1,0:T(8,128)} subtract(f32[2,256,256]{2,1,0:T(8,128)} %probe_in.1, f32[2,256,256]{2,1,0:T(8,128)S(1)} %get-tuple-element.5) | non-fusion elementwise | flops 131072 | bytes 1572864 | tf_op jit(solution)/shard_map/sub | solution.py:454

commit v3 on v2

--- a/solution.py
+++ b/solution.py
@@ -70,11 +70,15 @@
         p = self.p
         n = dg * p.H + dk
         sign = -1 if arriving else 1
-        k = lax.rem(p.k + sign * dk + p.H, p.H)
-        s = lax.rem(p.s + sign * dg + p.gs, p.gs)
-        slot = self.full.at[p.h, s, k] if arriving else self.full.at[p.h, p.s, p.k]
-        return remote(slot, slot, self.sems[4].at[n], self.sems[5].at[n],
-                      2 * k + p.h, p.g - p.s + s)
+        if dg == 0:
+            k = lax.rem(p.k + sign * dk + p.H, p.H)
+            slot = self.full.at[p.h, p.s, k if arriving else p.k]
+            to, group = 2 * k + p.h, p.g
+        else:
+            s = lax.rem(p.s + sign * dg + p.gs, p.gs)
+            slot = self.full.at[p.h, s if arriving else p.s, lax.rem(p.k - dk + p.H, p.H)]
+            to, group = 2 * p.k + p.h, p.g - p.s + s
+        return remote(slot, slot, self.sems[4].at[n], self.sems[5].at[n], to, group)
 
     def relay_copy(self, dg, dk, arriving):
         p = self.p
@@ -110,14 +114,24 @@
             self.spread_copy(d).wait()
             total = total + self.came[d - 1]
         self.full[p.h, p.s, p.k] = total
-        for dg, dk in self.others():
-            self.collect_copy(dg, dk, False).start()
+        for dk in range(1, p.H):
+            self.collect_copy(0, dk, False).start()
+        for dg in range(1, p.gs):
+            self.collect_copy(dg, 0, False).start()
         self.relay_copy(0, 0, False).start()
 
     def relay(self):
-        for dg, dk in self.others():
-            self.collect_copy(dg, dk, True).wait_recv()
-            self.relay_copy(dg, dk, False).start()
+        p = self.p
+        for dk in range(p.H):
+            if dk > 0:
+                self.collect_copy(0, dk, True).wait_recv()
+                for dg in range(1, p.gs):
+                    self.collect_copy(dg, dk, False).start()
+                self.relay_copy(0, dk, False).start()
+        for dk in range(p.H):
+            for dg in range(1, p.gs):
+                self.collect_copy(dg, dk, True).wait_recv()
+                self.relay_copy(dg, dk, False).start()
 
     def finish(self):
         self.relay_copy(0, 0, True).wait_recv()
@@ -138,15 +152,15 @@
 
 def kernel(T, G, gs, row_in, column_in, live_in, obj, probe_in, amp, *args):
     tables_in, args = args[:4], args[4:]
-    (obj_step, probe_step, scal_in, probe, *args) = args
+    (new_obj, new_probe, scal_in, probe, *args) = args
     (a_head, a_tail, b_head, b_tail, load_sem, far), args = args[:6], args[6:]
     body(T, G, gs, (row_in, column_in, live_in), (obj, probe_in, amp, *tables_in),
          (probe, a_head, a_tail, b_head, b_tail), load_sem, far, scal_in, probe, a_head, a_tail,
-         b_head, b_tail, obj_step, probe_step, *args)
+         b_head, b_tail, new_obj, new_probe, *args)
 
 
 def body(T, G, gs, scalars, inputs, loaded, load_sem, far, scal_in, probe, a_head, a_tail, b_head,
-         b_tail, obj_step, probe_step, pad, amps, scal_all, win, terms, light_terms, acc, acc_light,
+         b_tail, new_obj, new_probe, pad, amps, scal_all, win, terms, light_terms, acc, acc_light,
            edge, edge_light, grad_sum, *rest):
     t, g = lax.axis_index("tile"), lax.axis_index("group")
     obj, probe_in, amp, *tables_in = inputs
@@ -173,7 +187,7 @@
     count = 0
     for dt in range(T):
         for dg in range(G):
-            if (dt or dg) and (dt == 0 or (dt % 2 == 0 and (G == gs or dg == 0))):
+            if (dt or dg) and (dt == 0 or (dt % 2 == 0 and dg == 0)):
                 pl.semaphore_signal(
                     barrier, inc=1,
                     device_id={"tile": lax.rem(t + dt, T), "group": lax.rem(g + dg, G)},
@@ -372,14 +386,14 @@
         pl.when(not_first)(lambda: edge_copy(src, dst, True, base, True).wait_recv())
     below = 1.0 / (acc_light[1] + edge_light[0] + edge_light[1] + 0.25 * light_max)
     for ch in range(2):
-        obj_step[ch] = (acc[1, ch] + edge[0, ch] + edge[1, ch]) * below
+        new_obj[ch] = own[ch] - (acc[1, ch] + edge[0, ch] + edge[1, ch]) * below
     light_red.finish()
     light = light_red.get(0)
     below = 1.0 / (light + 0.25 * jnp.mean(light) + 1e-05)
     grad_red.relay()
     grad_red.finish()
     for ch in range(2):
-        probe_step[ch] = grad_red.get(ch) * below
+        new_probe[ch] = probe[ch] - grad_red.get(ch) * below
 
     for j in range(1, G):
         for ch in range(2):
@@ -395,6 +409,15 @@
         pl.when(not_last)(lambda: edge_copy(src, dst, True, base, False).wait_send())
 
 
+def put(obj, probe, obj_out, probe_out, sems):
+    copies = [pltpu.make_async_copy(obj, obj_out, sems.at[0]),
+              pltpu.make_async_copy(probe, probe_out, sems.at[1])]
+    for copy in copies:
+        copy.start()
+    for copy in copies:
+        copy.wait()
+
+
 def local(T, G, object_field, probe_field, amplitudes, row_start, column_start, live_slots):
     R, B = object_field.shape[1:]
     W = probe_field.shape[1]
@@ -420,7 +443,7 @@
     smem = pl.BlockSpec(memory_space=pltpu.SMEM)
     hbm = pl.BlockSpec(memory_space=pltpu.HBM)
     vmem = pl.BlockSpec(memory_space=pltpu.VMEM)
-    obj_step, probe_step = pl.pallas_call(
+    new_obj, new_probe = pl.pallas_call(
         functools.partial(kernel, T, G, gs),
         out_shape=(pltpu.VMEM(object_field.shape, F32), pltpu.VMEM(probe_field.shape, F32)),
         in_specs=[smem] * 3 + [hbm] * 7,
@@ -451,7 +474,16 @@
             collective_id=0, has_side_effects=True, vmem_limit_bytes=vmem_limit),
     )(row_start, column_start, live_slots, object_field, probe_field, amplitudes, head, tail,
       head.T, tail.T)
-    return object_field - obj_step, probe_field - probe_step
+    anywhere = pl.BlockSpec(memory_space=pl.ANY)
+    return pl.pallas_call(
+        put,
+        out_shape=(jax.ShapeDtypeStruct(object_field.shape, F32),
+                   jax.ShapeDtypeStruct(probe_field.shape, F32)),
+        in_specs=[vmem] * 2,
+        out_specs=(anywhere, anywhere),
+        scratch_shapes=[dma(2)],
+        compiler_params=pltpu.CompilerParams(vmem_limit_bytes=1024 * 1024),
+    )(new_obj, new_probe)
 
 
 def solution(mesh):

time: 48 us -> 45.2 us (0.942)
  other arithmetic: 3.5 us -> 0 us
  Pallas kernels: 41.7 us -> 42.4 us
    sub x2 -> x0, other arithmetic: 3.5 us -> none  [local(): return (object_field - obj_step, probe_field - probe_step)]
    pallas_call x0 -> x1, Pallas kernels: none -> 0.87 us  [local(): pl.pallas_call(put, out_shape=(jax.ShapeDtypeStruct(object_field.shape, F...]
where the time goes in v3:
time: 45.2 us; the launch traced here: 45 us
  Pallas kernels  42.4 us (94%)
  between operations  2.58 us (6%)
    pallas_call x1, Pallas kernels, local(): pl.pallas_call(functools.partial(kernel, T, G, gs), out_shape=(pltpu.VMEM...  41.6 us

profile of v3, /device:TPU:0, one launch (start us, length us, event | category | flops | bytes accessed | tf_op | source)
XLA Modules:
  0.0 45.0 jit_solution(3763735085137760261)
XLA Ops:
  2.6 41.6 %shard_map.113 = (f32[2,160,128]{2,1,0:T(8,128)S(1)}, f32[2,256,256]{2,1,0:T(8,128)S(1)}) custom-call(s32[1]{0:T(128)S(6)} %copy.12.row_in, s32[1]{0:T(128)S(6)} %copy.13.column_in, s32[1]{0:T(128)S(6)} %copy.14.live_in, f32[2,160,128]{2,1,0:T(8,128)} %obj.1, f32[2,256,256]{2,1,0:T(8,128)} %probe_in.1, f32[1,256,256]{2,1,0:T(8,128)} %amp.1, ...), custom_call_target="tpu_custom_call" | custom-call | tf_op jit(solution)/shard_map/pallas_call | solution.py:446
  44.1 0.9 %shard_map.114 = (f32[2,160,128]{2,1,0:T(8,128)}, f32[2,256,256]{2,1,0:T(8,128)}) custom-call(f32[2,160,128]{2,1,0:T(8,128)S(1)} %get-tuple-element.4.obj, f32[2,256,256]{2,1,0:T(8,128)S(1)} %get-tuple-element.5.probe), custom_call_target="tpu_custom_call" | custom-call | tf_op jit(solution)/shard_map/pallas_call | solution.py:478

commit v4 on v3

--- a/solution.py
+++ b/solution.py
@@ -203,7 +203,6 @@
     edges_here = (t > 0).astype(jnp.int32) + (t < T - 1).astype(jnp.int32)
     pl.semaphore_wait(barrier, count + edges_here)
     loads[0].wait()
-    loads[1].wait()
 
     def span(group):
         return pl.ds(pl.multiple_of(group * R, 8), R)
@@ -243,14 +242,15 @@
 
     not_first, not_last = t > 0, t < T - 1
 
+    for j in range(1, G):
+        scal_copy(j, False).start()
     for ch in range(2):
         for j in range(1, G):
             to_peer(j, ch, False).start()
     for ch in range(2):
         pl.when(not_first)(lambda: to_side(0, ch, False, False).start())
         pl.when(not_last)(lambda: to_side(0, ch, True, False).start())
-    for j in range(1, G):
-        scal_copy(j, False).start()
+    loads[1].wait()
     for j in range(1, G):
         amp_copy(j, False).start()
 
@@ -285,30 +285,39 @@
     hold(light_terms, probe_light)
     light_max = jnp.max(probe_light) + 1e-06
 
+    def numbers(k):
+        return scal[k, 0, 0], scal[k, 1, 0], scal[k, 2, 0].astype(F32)
+
+    def placed(ref, row, column):
+        first = g * R + spare - row
+        pieces = [ref[b, pl.ds(first, R), :] for b in range(blocks)]
+        wide = jnp.concatenate(pieces + [jnp.zeros((R, 3 * B - W), F32)], axis=1)
+        return pltpu.roll(wide, column, 1)
+
+    acc[...] = jnp.zeros(acc.shape, F32)
+    acc_light[...] = jnp.zeros(acc_light.shape, F32)
+    grad_sum[...] = jnp.zeros(grad_sum.shape, F32)
+    for j in range(1, G):
+        scal_copy(j, True).wait_recv()
+
+    @pl.loop(0, G)
+    def _(k):
+        row, column, weight = numbers(k)
+        spread = weight * placed(light_terms, row, column)
+        for b in range(3):
+            acc_light[b] += spread[:, b * B:(b + 1) * B]
+
     for ch in range(2):
         for j in range(1, G):
             to_peer(j, ch, True).wait_recv()
             pl.when(not_first)(lambda: to_side(j, ch, False, False).start())
             pl.when(not_last)(lambda: to_side(j, ch, True, False).start())
-    for j in range(1, G):
-        scal_copy(j, True).wait_recv()
+    pl.when(not_first)(lambda: edge_copy(acc_light, edge_light, False, 0, False).start())
+    pl.when(not_last)(lambda: edge_copy(acc_light, edge_light, True, 0, False).start())
     for j in range(G):
         for ch in range(2):
             pl.when(not_last)(lambda: to_side(j, ch, False, True).wait_recv())
             pl.when(not_first)(lambda: to_side(j, ch, True, True).wait_recv())
-
-    def numbers(k):
-        return scal[k, 0, 0], scal[k, 1, 0], scal[k, 2, 0].astype(F32)
-
-    def placed(ref, row, column):
-        first = g * R + spare - row
-        pieces = [ref[b, pl.ds(first, R), :] for b in range(blocks)]
-        wide = jnp.concatenate(pieces + [jnp.zeros((R, 3 * B - W), F32)], axis=1)
-        return pltpu.roll(wide, column, 1)
-
-    acc[...] = jnp.zeros(acc.shape, F32)
-    acc_light[...] = jnp.zeros(acc_light.shape, F32)
-    grad_sum[...] = jnp.zeros(grad_sum.shape, F32)
 
     def look(j, light):
         k = lax.rem(g + j, G)
@@ -316,16 +325,11 @@
         for ch in range(2):
             wide = jnp.concatenate([pad[b, ch, pl.ds(row, W), :] for b in range(3)], axis=1)
             win[k, ch] = pltpu.roll(wide, lax.rem(3 * B - column, 3 * B), 1)[:, 0:W]
-        spread = weight * placed(light_terms, row, column)
-        for b in range(3):
-            acc_light[b] += spread[:, b * B:(b + 1) * B]
         return light + weight * (win[k, 0] * win[k, 0] + win[k, 1] * win[k, 1])
 
     light = lax.fori_loop(0, G, look, jnp.zeros((W, W), F32))
     light_red.put(0, light)
     light_red.start_pair()
-    pl.when(not_first)(lambda: edge_copy(acc_light, edge_light, False, 0, False).start())
-    pl.when(not_last)(lambda: edge_copy(acc_light, edge_light, True, 0, False).start())
 
     def forth(k):
         wr, wi = win[k, 0], win[k, 1]
@@ -337,7 +341,7 @@
         factor = 1.0 - amps[k] * lax.rsqrt(jnp.maximum(zr * zr + zi * zi, 0.0625))
         far[0:W], far[W:] = zr * factor, zi * factor
 
-    def back(k):
+    def back(k, final=False):
         row, column, weight = numbers(k)
         wr, wi = win[k, 0], win[k, 1]
         pr, pi = probe[0], probe[1]
@@ -345,10 +349,16 @@
         y = table_left(b_head[...], b_tail[...], x)
         z = table_right(jnp.concatenate([y[:W], y[W:]], axis=1), a_head[...], a_tail[...])
         mr, mi = z[:, :W] * weight, z[:, W:] * weight
+        sums = (grad_sum[0] + (wr * mr + wi * mi), grad_sum[1] + (wr * mi - wi * mr))
+        for ch in range(2):
+            if final:
+                grad_red.put(ch, sums[ch])
+            else:
+                grad_sum[ch] = sums[ch]
+        if final:
+            grad_red.start_pair()
         hold(terms.at[0], pr * mr + pi * mi)
         hold(terms.at[1], pr * mi - pi * mr)
-        grad_sum[0] += wr * mr + wi * mi
-        grad_sum[1] += wr * mi - wi * mr
         for ch in range(2):
             spread = placed(terms.at[ch], row, column)
             for b in range(3):
@@ -356,7 +366,7 @@
 
     forth(g)
     light_red.start_spread()
-    back(g)
+    back(g, G == 1)
     for j in range(1, G):
         amp_copy(j, True).wait_recv()
 
@@ -368,29 +378,26 @@
         forth(lax.rem(g + 1, G))
         light_red.start_collect()
         pl.loop(1, G - 1)(both)
-        back(lax.rem(g + G - 1, G))
+        back(lax.rem(g + G - 1, G), True)
     else:
         light_red.start_collect()
 
-    for ch in range(2):
-        grad_red.put(ch, grad_sum[ch])
-    grad_red.start_pair()
+    grad_red.start_spread()
     pl.when(not_first)(lambda: edge_copy(acc, edge, False, 2, False).start())
     pl.when(not_last)(lambda: edge_copy(acc, edge, True, 2, False).start())
-    grad_red.start_spread()
     light_red.relay()
     grad_red.start_collect()
 
-    for src, dst, base in ((acc_light, edge_light, 0), (acc, edge, 2)):
-        pl.when(not_last)(lambda: edge_copy(src, dst, False, base, True).wait_recv())
-        pl.when(not_first)(lambda: edge_copy(src, dst, True, base, True).wait_recv())
-    below = 1.0 / (acc_light[1] + edge_light[0] + edge_light[1] + 0.25 * light_max)
-    for ch in range(2):
-        new_obj[ch] = own[ch] - (acc[1, ch] + edge[0, ch] + edge[1, ch]) * below
     light_red.finish()
     light = light_red.get(0)
     below = 1.0 / (light + 0.25 * jnp.mean(light) + 1e-05)
     grad_red.relay()
+    for src, dst, base in ((acc_light, edge_light, 0), (acc, edge, 2)):
+        pl.when(not_last)(lambda: edge_copy(src, dst, False, base, True).wait_recv())
+        pl.when(not_first)(lambda: edge_copy(src, dst, True, base, True).wait_recv())
+    share = 1.0 / (acc_light[1] + edge_light[0] + edge_light[1] + 0.25 * light_max)
+    for ch in range(2):
+        new_obj[ch] = own[ch] - (acc[1, ch] + edge[0, ch] + edge[1, ch]) * share
     grad_red.finish()
     for ch in range(2):
         new_probe[ch] = probe[ch] - grad_red.get(ch) * below

time: 45.2 us -> 45.2 us (level)
  no operation moved by 1% of the time
where the time goes in v4:
time: 45.2 us; the launch traced here: 45 us
  Pallas kernels  42.4 us (94%)
  between operations  2.58 us (6%)
    pallas_call x1, Pallas kernels, local(): pl.pallas_call(functools.partial(kernel, T, G, gs), out_shape=(pltpu.VMEM...  41.6 us

profile of v4, /device:TPU:0, one launch (start us, length us, event | category | flops | bytes accessed | tf_op | source)
XLA Modules:
  0.0 45.0 jit_solution(13995639981691328636)
XLA Ops:
  2.6 41.6 %shard_map.113 = (f32[2,160,128]{2,1,0:T(8,128)S(1)}, f32[2,256,256]{2,1,0:T(8,128)S(1)}) custom-call(s32[1]{0:T(128)S(6)} %copy.12.row_in, s32[1]{0:T(128)S(6)} %copy.13.column_in, s32[1]{0:T(128)S(6)} %copy.14.live_in, f32[2,160,128]{2,1,0:T(8,128)} %obj.1, f32[2,256,256]{2,1,0:T(8,128)} %probe_in.1, f32[1,256,256]{2,1,0:T(8,128)} %amp.1, ...), custom_call_target="tpu_custom_call" | custom-call | tf_op jit(solution)/shard_map/pallas_call | solution.py:453
  44.2 0.9 %shard_map.114 = (f32[2,160,128]{2,1,0:T(8,128)}, f32[2,256,256]{2,1,0:T(8,128)}) custom-call(f32[2,160,128]{2,1,0:T(8,128)S(1)} %get-tuple-element.4.obj, f32[2,256,256]{2,1,0:T(8,128)S(1)} %get-tuple-element.5.probe), custom_call_target="tpu_custom_call" | custom-call | tf_op jit(solution)/shard_map/pallas_call | solution.py:485
